TPU v7x, 512 devices: a whole 4x4x16 slice. The times are simulated.
512 devices in a mesh: mem: 16 (over z_lo, core), lat: 32 (over x, y, z_hi).
Axes of the slice: x: 4, y: 4, z: 16 (z_hi: 2, z_lo: 8; z = z_hi * 8 + z_lo), core: 2. Of those that a mesh axis runs over, the one named last changes fastest.
Arguments:
- control: bfloat16 [32, 10, 704, 1440], P('mem', None, 'lat'), may hold values from -6 to 6
- perturb: bfloat16 [32, 10, 704, 1440], P('mem', None, None, 'lat'), may hold values from -6 to 6
- lon_loc: bfloat16 [1440, 1440], P(None, 'mem'), may hold values from 0 to 1, as said below
- lat_loc: bfloat16 [704, 704], P('mem'), may hold values from 0 to 1, as said below
- static_scale: float32 [10, 704, 1440], P(None, 'mem', 'lat'), may hold values from 0.3 to 1
- static_field: float32 [10, 704, 1440], P(None, 'mem', 'lat'), may hold values from -6 to 6
- courant: float32 [2, 704, 1440], P(None, 'mem', 'lat'), may hold values from -0.48 to 0.48
Outputs:
- increment: float32 [10, 704, 1440], P(None, 'mem', 'lat')
- evolved: float32 [10, 704, 1440], P(None, 'mem', 'lat')
Inputs may be any that keep to these rules, and one draw needn't show every extreme that they name: `lon_loc`: Symmetric, with positive entries. `lat_loc`: Symmetric, with positive entries.
All inputs are finite; a program needn't handle non-finite values.
Results may differ from a plain program's by a relative error of at most 0.0027.
Values may be sent and summed in bfloat16 or wider, within the bound.
A program may use at most 64 MiB of HBM per device.

v0:
```python
import math
import jax
import jax.numpy as jnp
from jax import lax
from jax.sharding import PartitionSpec as P

NLAT = 704
STEPS = 4


def padded_2(shard, sides, width, wrap):
    for axis, dim in sides:
        size, length = (lax.axis_size(axis), shard.shape[dim])
        up = [(i, (i + 1) % size) for i in range(size if wrap else size - 1)]
        down = [(j, i) for i, j in up]
        last = lax.slice_in_dim(shard, length - width, length, axis=dim)
        leading = lax.slice_in_dim(shard, 0, width, axis=dim)
        before = lax.ppermute(last, axis, up)
        after = lax.ppermute(leading, axis, down)
        shard = jnp.concatenate([before, shard, after], axis=dim)
    return shard


def in_order(parts, dim):
    shape = list(parts.shape[1:])
    shape[dim] *= parts.shape[0]
    return jnp.moveaxis(parts, 0, dim).reshape(shape)


def sent_to_all(shard, axis):
    length = lax.axis_size(axis)
    return lax.all_to_all(
        jnp.broadcast_to(shard[None], (length, *shard.shape)), axis, 0, 0, tiled=True
    )


def collect(shard, axis, dim):
    return in_order(sent_to_all(shard, axis), dim)


def upwind(padded, east_west, north_south):
    center = padded[:, 1:-1, 1:-1]
    western = padded[:, 1:-1, :-2]
    eastern = padded[:, 1:-1, 2:]
    southern = padded[:, :-2, 1:-1]
    northern = padded[:, 2:, 1:-1]
    zonal = jnp.maximum(east_west, 0.0) * (center - western) + jnp.minimum(east_west, 0.0) * (
        eastern - center
    )
    meridional = jnp.maximum(north_south, 0.0) * (center - southern) + jnp.minimum(
        north_south, 0.0
    ) * (northern - center)
    return center - zonal - meridional


def lon_rim(values, width):
    return padded_2(values, (("lat", 2),), width, True)


def lat_rim(values, width):
    return padded_2(values, (("mem", 1),), width, False)


def evolve(current, courant):
    fields = current.shape[0]
    stacked = jnp.concatenate([current, courant], axis=0)
    extended = lat_rim(lon_rim(stacked, STEPS), STEPS)
    result = extended[:fields]
    wind_ext = extended[fields:]
    for step_index in range(STEPS):
        margin = step_index + 1
        inner_wind = wind_ext[
            :, margin : wind_ext.shape[1] - margin, margin : wind_ext.shape[2] - margin
        ]
        result = upwind(result, inner_wind[0], inner_wind[1])
    return result


def per_device(control, perturb, lon_loc, lat_loc, static_scale, static_field, courant):
    along_lon = jnp.einsum(
        "mfal,lc->amfc",
        control,
        lax.all_gather(lon_loc, "mem", axis=1, tiled=True),
        preferred_element_type=jnp.float32,
    ).astype(jnp.bfloat16)
    banded = lax.all_to_all(along_lon, "lat", split_axis=3, concat_axis=0, tiled=True)
    mem_here = banded.shape[1]
    fields = banded.shape[2]
    lon_width = banded.shape[3]
    flat_band = banded.reshape(banded.shape[0], mem_here * fields * lon_width)
    pert_rows = jnp.transpose(perturb, (2, 0, 1, 3))
    lat_weights_all = collect(lat_loc, "mem", 0)
    members = mem_here * lax.axis_size("mem")
    ens_scale = 1.0 / math.sqrt(members - 1)
    rows_own = NLAT // lax.axis_size("mem")
    localized = jnp.dot(lat_weights_all, flat_band, preferred_element_type=jnp.float32)
    localized = localized.reshape(NLAT, mem_here, fields, lon_width)
    ensemble_all = jnp.transpose(
        lax.psum(jnp.sum(localized * pert_rows.astype(jnp.float32), axis=1) * ens_scale, "mem"),
        (1, 0, 2),
    )
    offset = lax.axis_index("mem") * rows_own
    ensemble = lax.dynamic_slice_in_dim(ensemble_all, offset, rows_own, 1)
    increment = ensemble + static_scale * static_field
    evolved = evolve(increment, courant)
    return (increment, evolved)


def solution(mesh):
    placed = (
        P("mem", None, "lat", None),
        P("mem", None, None, "lat"),
        P(None, "mem"),
        P("mem", None),
        P(None, "mem", "lat"),
        P(None, "mem", "lat"),
        P(None, "mem", "lat"),
    )
    return jax.shard_map(
        per_device,
        mesh=mesh,
        in_specs=placed,
        out_specs=(P(None, "mem", "lat"), P(None, "mem", "lat")),
        check_vma=False,
    )
```

profile of v0, /device:TPU:1, one launch (start us, length us, event | category | flops | bytes accessed | tf_op | source)
XLA Modules:
  0.0 541.9 jit_solution(11255603198932027136)
XLA Ops:
  7.2 0.0 all-gather.3.cloned.1.call-start
  7.2 0.7 all-gather.3.cloned.1.call-update
  7.9 2.0 broadcast_in_dim.2
  9.9 14.0 %all-to-all-start.1 = ((bf16[16,44,704]{2,1,0:T(8,128)(2,1)}), bf16[16,44,704]{2,1,0:T(8,128)(2,1)S(1)}, u32[]{:S(2)}, u32[]{:S(2)}) async-start(bf16[16,44,704]{2,1,0:T(8,128)(2,1)} %broadcast_in_dim.2), calls=%async_computation.1 | async-start | bytes 2359296 | tf_op jit(solution)/shard_map/all_to_all | solution.py:32
  23.9 111.8 %all-gather.3.cloned.1.call-done = bf16[16,90,1440]{2,1,0:T(8,128)(2,1)} async-done(((bf16[1,90,1440]{2,1,0:T(8,128)(2,1)}), bf16[16,90,1440]{2,1,0:T(8,128)(2,1)}) %all-gather.3.cloned.1.call-update) | async-done | bytes 4147216 | tf_op jit(solution)/shard_map/all_gather | solution.py:83
  135.8 5.9 %reshape.20 = bf16[1440,1440,1,1]{1,0,2,3:T(8,128)(2,1)} reshape(bf16[16,90,1440]{2,1,0:T(8,128)(2,1)} %all-gather.3.cloned.1.call-done) | data formatting | bytes 8294400
  141.7 6.0 %fusion.6 = bf16[22,2,10,1440]{3,0,2,1:T(8,128)(2,1)} fusion(bf16[1440,1440,1,1]{1,0,2,3:T(8,128)(2,1)} %reshape.20, bf16[2,10,22,1440]{3,0,2,1:T(2,128)(2,1)S(1)} %copy-done), kind=kOutput, calls=%fused_computation.5 | convolution fusion | flops 1825401600 | bytes 6681600 | tf_op jit(solution)/shard_map/mfal,lc->amfc/dot_general | solution.py:80
  147.7 15.6 %copy.36 = bf16[22,2,10,1440]{0,1,2,3:T(2,128)(2,1)} copy(bf16[22,2,10,1440]{3,0,2,1:T(8,128)(2,1)} %fusion.6) | data formatting | bytes 2534400 | tf_op jit(solution)/shard_map/convert_element_type | solution.py:85
  163.3 11.0 %reshape.22 = bf16[32,2,9900]{2,1,0:T(2,128)(2,1)} reshape(bf16[1440,10,2,22]{3,2,1,0:T(2,128)(2,1)} %bitcast.62) | data formatting | bytes 2534400
  174.3 1.0 copy-done.1
  175.3 12.5 %all-to-all-start = ((bf16[32,2,9900]{2,1,0:T(2,128)(2,1)}), bf16[32,2,9900]{2,1,0:T(2,128)(2,1)S(1)}, u32[]{:S(2)}, u32[]{:S(2)}) async-start(bf16[32,2,9900]{2,1,0:T(2,128)(2,1)} %reshape.22), calls=%async_computation | async-start | bytes 2555904 | tf_op jit(solution)/shard_map/all_to_all | solution.py:86
  187.8 0.0 all-reduce.2.cloned.1.call-start
  187.9 2.3 reshape.16
  190.2 44.9 %all-to-all-done = bf16[32,2,9900]{2,1,0:T(2,128)(2,1)S(1)} async-done(((bf16[32,2,9900]{2,1,0:T(2,128)(2,1)}), bf16[32,2,9900]{2,1,0:T(2,128)(2,1)S(1)}, u32[]{:S(2)}, u32[]{:S(2)}) %all-to-all-start) | async-done | bytes 1267232 | tf_op jit(solution)/shard_map/all_to_all | solution.py:86
  235.1 7.4 %reshape.23 = bf16[1440,10,2,22]{3,2,1,0:T(2,128)(2,1)} reshape(bf16[32,2,9900]{2,1,0:T(2,128)(2,1)S(1)} %all-to-all-done) | data formatting | bytes 2534400
  242.5 25.1 %copy.53 = bf16[22,2,10,32,45]{4,2,1,0,3:T(8,128)(2,1)} copy(bf16[22,2,10,32,45]{0,1,2,4,3:T(2,128)(2,1)} %bitcast.61) | data formatting | bytes 2534400 | tf_op jit(solution)/shard_map/all_to_all | solution.py:86
  267.6 7.9 %reshape.15 = bf16[704,900]{1,0:T(8,128)(2,1)S(1)} reshape(bf16[32,22,2,10,45]{4,3,2,1,0:T(8,128)(2,1)} %bitcast.63) | data formatting | bytes 2534400 | tf_op jit(solution)/shard_map/reshape | solution.py:90
  275.5 4.3 convolution_bitcast_fusion
  279.8 3.9 reshape.17
  283.7 2.5 fusion.2
  286.2 1.2 broadcast_multiply_fusion
  287.5 0.9 copy-done.3
  288.4 0.2 copy.40
  288.6 0.2 copy.41
  288.8 0.1 copy.42
  288.9 206.1 %all-reduce.2.cloned.1.call-done = f32[704,10,45]{0,2,1:T(8,128)} async-done(((f32[704,10,45]{0,2,1:T(8,128)}), f32[704,10,45]{0,2,1:T(8,128)}) %all-reduce.2.cloned.1.call-update) | async-done | bytes 1267216 | tf_op jit(solution)/shard_map/psum | solution.py:99
  495.0 1.2 bitcast_add_fusion
  496.2 8.1 %collective-permute-start = (f32[12,44,4]{1,2,0:T(4,128)S(1)}, f32[12,44,4]{1,2,0:T(4,128)S(1)}, u32[]{:S(2)}, u32[]{:S(2)}) collective-permute-start(f32[12,44,4]{1,2,0:T(4,128)S(1)} %get-tuple-element.26), channel_id=1, source_target_pairs={{0,1},{1,2},{2,3},{3,4},{4,5},{5,6},{6,7},{7,8},{8,9},{9,10},{10,1... | collective-permute-start | bytes 25352 | tf_op jit(solution)/shard_map/ppermute | solution.py:18
  504.4 10.1 %collective-permute-start.1 = (f32[12,44,4]{1,2,0:T(4,128)S(1)}, f32[12,44,4]{1,2,0:T(4,128)S(1)}, u32[]{:S(2)}, u32[]{:S(2)}) collective-permute-start(f32[12,44,4]{1,2,0:T(4,128)S(1)} %get-tuple-element.27), channel_id=1, source_target_pairs={{1,0},{2,1},{3,2},{4,3},{5,4},{6,5},{7,6},{8,7},{9,8},{10,9},{11,1... | collective-permute-start | bytes 25352 | tf_op jit(solution)/shard_map/ppermute | solution.py:19
  514.5 3.4 collective-permute-done.1
  517.9 0.1 pad_maximum_fusion
  518.0 0.2 fusion.42
  518.2 4.9 collective-permute-start.2
  523.1 7.6 %collective-permute-start.3 = (f32[12,4,53]{1,2,0:T(8,128)S(1)}, f32[12,4,53]{1,2,0:T(8,128)S(1)}, u32[]{:S(2)}, u32[]{:S(2)}) collective-permute-start(f32[12,4,53]{1,2,0:T(8,128)S(1)} %get-tuple-element.25), channel_id=1, source_target_pairs={{32,0},{64,32},{96,64},{128,96},{160,128},{192,160},{224,192},{256... | collective-permute-start | bytes 30536 | tf_op jit(solution)/shard_map/ppermute | solution.py:19
  530.8 0.1 copy.44
  530.9 0.1 copy.45
  531.0 0.1 copy.47
  531.1 0.1 copy.48
  531.2 0.9 copy.49
  532.0 0.1 maximum_bitcast_fusion.7
  532.2 0.1 maximum_bitcast_fusion.1
  532.3 0.1 maximum_bitcast_fusion.3
  532.5 0.3 pad_maximum_fusion.1
  532.7 0.4 fusion.20
  533.1 0.4 fusion.12
  533.5 0.3 fusion.36
  533.8 0.3 fusion.28
  534.2 0.9 copy.50
  (21 shorter events, 0.1 us)
Async XLA Ops:
  7.2 134.5 %copy-start = (bf16[2,10,22,1440]{3,0,2,1:T(2,128)(2,1)S(1)}, bf16[2,10,22,1440]{3,0,2,1:T(2,128)(2,1)}, u32[]{:S(2)}) copy-start(bf16[2,10,22,1440]{3,0,2,1:T(2,128)(2,1)} %param.7) | copy-start | bytes 3801604
  7.2 128.6 %all-gather.3.cloned.1.call-start = ((), (), s32[]{:S(2)}) async-start(), calls=%async_computation.3 | async-start | bytes 5013504 | tf_op jit(solution)/shard_map/all_gather | solution.py:83
  9.9 164.4 %all-to-all-start.1 = ((bf16[16,44,704]{2,1,0:T(8,128)(2,1)}), bf16[16,44,704]{2,1,0:T(8,128)(2,1)S(1)}, u32[]{:S(2)}, u32[]{:S(2)}) async-start(bf16[16,44,704]{2,1,0:T(8,128)(2,1)} %broadcast_in_dim.2), calls=%async_computation.1 | async-start | bytes 2359296 | tf_op jit(solution)/shard_map/all_to_all | solution.py:32
  174.3 1.0 copy-start.1
  175.3 59.7 %all-to-all-start = ((bf16[32,2,9900]{2,1,0:T(2,128)(2,1)}), bf16[32,2,9900]{2,1,0:T(2,128)(2,1)S(1)}, u32[]{:S(2)}, u32[]{:S(2)}) async-start(bf16[32,2,9900]{2,1,0:T(2,128)(2,1)} %reshape.22), calls=%async_computation | async-start | bytes 2555904 | tf_op jit(solution)/shard_map/all_to_all | solution.py:86
  187.8 307.2 %all-reduce.2.cloned.1.call-start = ((), (), s32[]{:S(2)}) async-start(), calls=%async_computation.2 | async-start | bytes 2949120 | tf_op jit(solution)/shard_map/psum | solution.py:99
  279.8 3.9 copy-start.2
  287.5 0.9 copy-start.3
  287.5 1.1 copy-start.4
  287.5 1.3 copy-start.5
  496.2 18.3 %collective-permute-start = (f32[12,44,4]{1,2,0:T(4,128)S(1)}, f32[12,44,4]{1,2,0:T(4,128)S(1)}, u32[]{:S(2)}, u32[]{:S(2)}) collective-permute-start(f32[12,44,4]{1,2,0:T(4,128)S(1)} %get-tuple-element.26), channel_id=1, source_target_pairs={{0,1},{1,2},{2,3},{3,4},{4,5},{5,6},{6,7},{7,8},{8,9},{9,10},{10,1... | collective-permute-start | bytes 25352 | tf_op jit(solution)/shard_map/ppermute | solution.py:18
  504.4 13.6 %collective-permute-start.1 = (f32[12,44,4]{1,2,0:T(4,128)S(1)}, f32[12,44,4]{1,2,0:T(4,128)S(1)}, u32[]{:S(2)}, u32[]{:S(2)}) collective-permute-start(f32[12,44,4]{1,2,0:T(4,128)S(1)} %get-tuple-element.27), channel_id=1, source_target_pairs={{1,0},{2,1},{3,2},{4,3},{5,4},{6,5},{7,6},{8,7},{9,8},{10,9},{11,1... | collective-permute-start | bytes 25352 | tf_op jit(solution)/shard_map/ppermute | solution.py:19
  518.2 13.9 %collective-permute-start.2 = (f32[12,4,53]{1,2,0:T(8,128)S(1)}, f32[12,4,53]{1,2,0:T(8,128)S(1)}, u32[]{:S(2)}, u32[]{:S(2)}) collective-permute-start(f32[12,4,53]{1,2,0:T(8,128)S(1)} %get-tuple-element.24), channel_id=1, source_target_pairs={{0,32},{32,64},{64,96},{96,128},{128,160},{160,192},{192,224},{224... | collective-permute-start | bytes 30536 | tf_op jit(solution)/shard_map/ppermute | solution.py:18
  523.1 8.9 %collective-permute-start.3 = (f32[12,4,53]{1,2,0:T(8,128)S(1)}, f32[12,4,53]{1,2,0:T(8,128)S(1)}, u32[]{:S(2)}, u32[]{:S(2)}) collective-permute-start(f32[12,4,53]{1,2,0:T(8,128)S(1)} %get-tuple-element.25), channel_id=1, source_target_pairs={{32,0},{64,32},{96,64},{128,96},{160,128},{192,160},{224,192},{256... | collective-permute-start | bytes 30536 | tf_op jit(solution)/shard_map/ppermute | solution.py:19
Sparse Core Ops, SparseCore 0:
  10.1 125.6 all-gather.2
  287.6 207.3 all-reduce.1
where the time goes:
time: 545 us; the launch traced here: 542 us
  waiting for transfers between devices  367 us (67%)
  local copies, waits for them, and re-layouts  86 us (16%)
  starting transfers between devices  57.4 us (11%)
  between operations  14.2 us (3%)
  matrix products  10.2 us (2%)
  other arithmetic  7.06 us (1%)
    psum x1, waiting for transfers between devices, per_device(): lax.psum(jnp.sum(localized * pert_rows.astype(jnp.float32), axis=1) * ens...  206 us
    all_gather x1, waiting for transfers between devices, per_device(): lax.all_gather(lon_loc, 'mem', axis=1, tiled=True)  112 us
    all_to_all x1, waiting for transfers between devices, per_device(): lax.all_to_all(along_lon, 'lat', split_axis=3, concat_axis=0, tiled=True)  44.9 us
    unnamed x20, local copies, waits for them, and re-layouts  28.6 us
    all_to_all x1, local copies, waits for them, and re-layouts, per_device(): lax.all_to_all(along_lon, 'lat', split_axis=3, concat_axis=0, tiled=True)  25.1 us
    ppermute x2, starting transfers between devices, padded_2(): after = lax.ppermute(leading, axis, down)  17.7 us
    convert_element_type x1, local copies, waits for them, and re-layouts, per_device(): along_lon = jnp.einsum('mfal,lc->amfc', control, lax.all_gather(lon_loc,...  15.6 us
    all_to_all x1, starting transfers between devices, sent_to_all(): lax.all_to_all(jnp.broadcast_to(shard[None], (length, *shard.shape)), axi...  14 us
  transfers between devices with their start and end apart: 8, of which 4 were waited for; matrix products, arithmetic and copies ran while one was open for 8% of the time, Pallas kernels for 0%

commit v1 on v0

--- a/solution.py
+++ b/solution.py
@@ -6,6 +6,11 @@
 
 NLAT = 704
 STEPS = 4
+
+
+def swapped_in(block, mesh_axis, dim):
+    sent = jnp.stack([block] * lax.axis_size(mesh_axis))
+    return jnp.concatenate(lax.all_to_all(sent, mesh_axis, 0, 0), axis=dim)
 
 
 def padded_2(shard, sides, width, wrap):
@@ -78,10 +83,7 @@
 
 def per_device(control, perturb, lon_loc, lat_loc, static_scale, static_field, courant):
     along_lon = jnp.einsum(
-        "mfal,lc->amfc",
-        control,
-        lax.all_gather(lon_loc, "mem", axis=1, tiled=True),
-        preferred_element_type=jnp.float32,
+        "mfal,lc->amfc", control, swapped_in(lon_loc, "mem", 1), preferred_element_type=jnp.float32
     ).astype(jnp.bfloat16)
     banded = lax.all_to_all(along_lon, "lat", split_axis=3, concat_axis=0, tiled=True)
     mem_here = banded.shape[1]

time: 545 us -> 666 us (1.22)
  blocking collectives: 0 us -> 221 us
  waiting for transfers between devices: 367 us -> 274 us
  starting transfers between devices: 57.4 us -> 49.9 us
    all_to_all x0 -> x1, blocking collectives: none -> 221 us  [swapped_in(): return jnp.concatenate(lax.all_to_all(sent, mesh_axis, 0, 0), axis=dim)]
    all_gather x1 -> x0, waiting for transfers between devices: 112 us -> none  [per_device(): lax.all_gather(lon_loc, 'mem', axis=1, tiled=True)]
    psum x1, waiting for transfers between devices: 206 us -> 233 us  [per_device(): lax.psum(jnp.sum(localized * pert_rows.astype(jnp.float32), axis=1) * ens...]
    all_to_all x1, waiting for transfers between devices: 44.9 us -> 27.3 us  [per_device(): lax.all_to_all(along_lon, 'lat', split_axis=3, concat_axis=0, tiled=True)]
    all_to_all x1, waiting for transfers between devices: 0.01 us -> 10.5 us  [sent_to_all(): lax.all_to_all(jnp.broadcast_to(shard[None], (length, *shard.shape)), axi...]
    all_to_all x1, starting transfers between devices: 14 us -> 6.27 us  [sent_to_all(): lax.all_to_all(jnp.broadcast_to(shard[None], (length, *shard.shape)), axi...]
    unnamed x20 -> x21, local copies, waits for them, and re-layouts: 28.6 us -> 22.7 us
  transfers between devices with their start and end apart: 8 -> 7, of which waited for: 4 -> 4; matrix products, arithmetic and copies ran while one was open for 8% -> 6% of each run, Pallas kernels for 0% -> 0%
where the time goes in v1:
time: 666 us; the launch traced here: 663 us
  waiting for transfers between devices  274 us (41%)
  blocking collectives  221 us (33%)
  local copies, waits for them, and re-layouts  86.6 us (13%)
  starting transfers between devices  49.9 us (7%)
  between operations  14.3 us (2%)
  matrix products  10.2 us (2%)
  other arithmetic  7.07 us (1%)
    psum x1, waiting for transfers between devices, per_device(): lax.psum(jnp.sum(localized * pert_rows.astype(jnp.float32), axis=1) * ens...  233 us
    all_to_all x1, blocking collectives, swapped_in(): return jnp.concatenate(lax.all_to_all(sent, mesh_axis, 0, 0), axis=dim)  221 us
    all_to_all x1, waiting for transfers between devices, per_device(): lax.all_to_all(along_lon, 'lat', split_axis=3, concat_axis=0, tiled=True)  27.3 us
    all_to_all x1, local copies, waits for them, and re-layouts, per_device(): lax.all_to_all(along_lon, 'lat', split_axis=3, concat_axis=0, tiled=True)  25.1 us
    unnamed x21, local copies, waits for them, and re-layouts  22.7 us
    ppermute x2, starting transfers between devices, padded_2(): after = lax.ppermute(leading, axis, down)  17.7 us
    convert_element_type x1, local copies, waits for them, and re-layouts, per_device(): along_lon = jnp.einsum('mfal,lc->amfc', control, swapped_in(lon_loc, 'mem...  15.6 us
  transfers between devices with their start and end apart: 7, of which 4 were waited for; matrix products, arithmetic and copies ran while one was open for 6% of the time, Pallas kernels for 0%

profile of v1, /device:TPU:1, one launch (start us, length us, event | category | flops | bytes accessed | tf_op | source)
XLA Modules:
  0.0 663.2 jit_solution(14590434603605455101)
XLA Ops:
  7.2 1.5 stack.2
  8.7 221.2 %all_to_all.25 = bf16[16,1440,90]{1,2,0:T(8,128)(2,1)} all-to-all(bf16[16,1440,90]{1,2,0:T(8,128)(2,1)S(1)} %stack.2), channel_id=1, replica_groups=mesh['mem'=16,'lat'=32] {'mem'}, dimensions={0} | all-to-all | bytes 8294400 | tf_op jit(solution)/shard_map/all_to_all | solution.py:13
  229.9 1.1 broadcast_in_dim.2
  231.0 6.3 all-to-all-start.2
  237.3 5.9 reshape.24
  243.2 5.9 fusion.6
  249.2 15.6 %copy.40 = bf16[22,2,10,1440]{0,1,2,3:T(2,128)(2,1)} copy(bf16[22,2,10,1440]{3,0,2,1:T(8,128)(2,1)} %fusion.6) | data formatting | bytes 2534400 | tf_op jit(solution)/shard_map/convert_element_type | solution.py:87
  264.8 11.1 %reshape.29 = bf16[32,2,9900]{2,1,0:T(2,128)(2,1)} reshape(bf16[1440,10,2,22]{3,2,1,0:T(2,128)(2,1)} %bitcast.62) | data formatting | bytes 2534400
  275.9 10.5 %all-to-all-done.2 = bf16[16,44,704]{2,1,0:T(8,128)(2,1)S(1)} async-done(((bf16[16,44,704]{2,1,0:T(8,128)(2,1)}), bf16[16,44,704]{2,1,0:T(8,128)(2,1)S(1)}, u32[]{:S(2)}, u32[]{:S(2)}) %all-to-all-start.2) | async-done | bytes 991264 | tf_op jit(solution)/shard_map/all_to_all | solution.py:37
  286.4 1.0 copy-done.1
  287.4 12.8 %all-to-all-start.1 = ((bf16[32,2,9900]{2,1,0:T(2,128)(2,1)}), bf16[32,2,9900]{2,1,0:T(2,128)(2,1)S(1)}, u32[]{:S(2)}, u32[]{:S(2)}) async-start(bf16[32,2,9900]{2,1,0:T(2,128)(2,1)} %reshape.29), calls=%async_computation.1 | async-start | bytes 2555904 | tf_op jit(solution)/shard_map/all_to_all | solution.py:88
  300.2 0.0 all-reduce.2.cloned.1.call-start
  300.2 2.3 reshape.26
  302.5 27.3 %all-to-all-done.1 = bf16[32,2,9900]{2,1,0:T(2,128)(2,1)S(1)} async-done(((bf16[32,2,9900]{2,1,0:T(2,128)(2,1)}), bf16[32,2,9900]{2,1,0:T(2,128)(2,1)S(1)}, u32[]{:S(2)}, u32[]{:S(2)}) %all-to-all-start.1) | async-done | bytes 1267232 | tf_op jit(solution)/shard_map/all_to_all | solution.py:88
  329.8 7.4 %reshape.30 = bf16[1440,10,2,22]{3,2,1,0:T(2,128)(2,1)} reshape(bf16[32,2,9900]{2,1,0:T(2,128)(2,1)S(1)} %all-to-all-done.1) | data formatting | bytes 2534400
  337.2 25.1 %copy.58 = bf16[22,2,10,32,45]{4,2,1,0,3:T(8,128)(2,1)} copy(bf16[22,2,10,32,45]{0,1,2,4,3:T(2,128)(2,1)} %bitcast.61) | data formatting | bytes 2534400 | tf_op jit(solution)/shard_map/all_to_all | solution.py:88
  362.3 7.9 %reshape.25 = bf16[704,900]{1,0:T(8,128)(2,1)S(1)} reshape(bf16[32,22,2,10,45]{4,3,2,1,0:T(8,128)(2,1)} %bitcast.63) | data formatting | bytes 2534400 | tf_op jit(solution)/shard_map/reshape | solution.py:92
  370.2 4.3 convolution_bitcast_fusion
  374.5 3.9 reshape.27
  378.4 2.5 fusion.2
  381.0 1.3 broadcast_multiply_fusion
  382.3 0.9 copy-done.3
  383.2 0.2 copy.44
  383.4 0.2 copy.45
  383.5 0.1 copy.46
  383.6 232.7 %all-reduce.2.cloned.1.call-done = f32[704,10,45]{0,2,1:T(8,128)} async-done(((f32[704,10,45]{0,2,1:T(8,128)}), f32[704,10,45]{0,2,1:T(8,128)}) %all-reduce.2.cloned.1.call-update) | async-done | bytes 1267216 | tf_op jit(solution)/shard_map/psum | solution.py:101
  616.4 1.2 bitcast_add_fusion
  617.6 8.1 %collective-permute-start = (f32[12,44,4]{1,2,0:T(4,128)S(1)}, f32[12,44,4]{1,2,0:T(4,128)S(1)}, u32[]{:S(2)}, u32[]{:S(2)}) collective-permute-start(f32[12,44,4]{1,2,0:T(4,128)S(1)} %get-tuple-element.26), channel_id=1, source_target_pairs={{0,1},{1,2},{2,3},{3,4},{4,5},{5,6},{6,7},{7,8},{8,9},{9,10},{10,1... | collective-permute-start | bytes 25352 | tf_op jit(solution)/shard_map/ppermute | solution.py:23
  625.7 10.1 %collective-permute-start.1 = (f32[12,44,4]{1,2,0:T(4,128)S(1)}, f32[12,44,4]{1,2,0:T(4,128)S(1)}, u32[]{:S(2)}, u32[]{:S(2)}) collective-permute-start(f32[12,44,4]{1,2,0:T(4,128)S(1)} %get-tuple-element.27), channel_id=1, source_target_pairs={{1,0},{2,1},{3,2},{4,3},{5,4},{6,5},{7,6},{8,7},{9,8},{10,9},{11,1... | collective-permute-start | bytes 25352 | tf_op jit(solution)/shard_map/ppermute | solution.py:24
  635.8 3.4 collective-permute-done.1
  639.3 0.1 pad_maximum_fusion
  639.3 0.2 fusion.42
  639.5 4.9 collective-permute-start.2
  644.4 7.6 %collective-permute-start.3 = (f32[12,4,53]{1,2,0:T(8,128)S(1)}, f32[12,4,53]{1,2,0:T(8,128)S(1)}, u32[]{:S(2)}, u32[]{:S(2)}) collective-permute-start(f32[12,4,53]{1,2,0:T(8,128)S(1)} %get-tuple-element.25), channel_id=1, source_target_pairs={{32,0},{64,32},{96,64},{128,96},{160,128},{192,160},{224,192},{256... | collective-permute-start | bytes 30536 | tf_op jit(solution)/shard_map/ppermute | solution.py:24
  652.1 0.1 copy.48
  652.2 0.1 copy.49
  652.3 0.1 copy.51
  652.4 0.1 copy.52
  652.5 0.9 copy.53
  653.4 0.1 maximum_bitcast_fusion.7
  653.5 0.1 maximum_bitcast_fusion.1
  653.6 0.1 maximum_bitcast_fusion.3
  653.8 0.3 pad_maximum_fusion.1
  654.1 0.4 fusion.20
  654.4 0.4 fusion.12
  654.8 0.3 fusion.36
  655.2 0.3 fusion.28
  655.5 0.9 copy.54
  (22 shorter events, 0.1 us)
Async XLA Ops:
  7.2 236.1 %copy-start = (bf16[2,10,22,1440]{3,0,2,1:T(2,128)(2,1)S(1)}, bf16[2,10,22,1440]{3,0,2,1:T(2,128)(2,1)}, u32[]{:S(2)}) copy-start(bf16[2,10,22,1440]{3,0,2,1:T(2,128)(2,1)} %param.7) | copy-start | bytes 3801604
  8.7 221.2 %copy-start.6 = (bf16[44,704]{1,0:T(8,128)(2,1)S(1)}, bf16[44,704]{1,0:T(8,128)(2,1)}, u32[]{:S(2)}) copy-start(bf16[44,704]{1,0:T(8,128)(2,1)} %param.10) | copy-start | bytes 185860
  231.0 55.3 %all-to-all-start.2 = ((bf16[16,44,704]{2,1,0:T(8,128)(2,1)}), bf16[16,44,704]{2,1,0:T(8,128)(2,1)S(1)}, u32[]{:S(2)}, u32[]{:S(2)}) async-start(bf16[16,44,704]{2,1,0:T(8,128)(2,1)} %broadcast_in_dim.2), calls=%async_computation.2 | async-start | bytes 2359296 | tf_op jit(solution)/shard_map/all_to_all | solution.py:37
  286.4 1.0 copy-start.1
  287.4 42.4 %all-to-all-start.1 = ((bf16[32,2,9900]{2,1,0:T(2,128)(2,1)}), bf16[32,2,9900]{2,1,0:T(2,128)(2,1)S(1)}, u32[]{:S(2)}, u32[]{:S(2)}) async-start(bf16[32,2,9900]{2,1,0:T(2,128)(2,1)} %reshape.29), calls=%async_computation.1 | async-start | bytes 2555904 | tf_op jit(solution)/shard_map/all_to_all | solution.py:88
  300.2 316.2 %all-reduce.2.cloned.1.call-start = ((), (), s32[]{:S(2)}) async-start(), calls=%async_computation.3 | async-start | bytes 2949120 | tf_op jit(solution)/shard_map/psum | solution.py:101
  374.5 3.9 copy-start.2
  382.2 0.9 copy-start.3
  382.2 1.1 copy-start.4
  382.2 1.3 copy-start.5
  617.6 18.3 %collective-permute-start = (f32[12,44,4]{1,2,0:T(4,128)S(1)}, f32[12,44,4]{1,2,0:T(4,128)S(1)}, u32[]{:S(2)}, u32[]{:S(2)}) collective-permute-start(f32[12,44,4]{1,2,0:T(4,128)S(1)} %get-tuple-element.26), channel_id=1, source_target_pairs={{0,1},{1,2},{2,3},{3,4},{4,5},{5,6},{6,7},{7,8},{8,9},{9,10},{10,1... | collective-permute-start | bytes 25352 | tf_op jit(solution)/shard_map/ppermute | solution.py:23
  625.7 13.6 %collective-permute-start.1 = (f32[12,44,4]{1,2,0:T(4,128)S(1)}, f32[12,44,4]{1,2,0:T(4,128)S(1)}, u32[]{:S(2)}, u32[]{:S(2)}) collective-permute-start(f32[12,44,4]{1,2,0:T(4,128)S(1)} %get-tuple-element.27), channel_id=1, source_target_pairs={{1,0},{2,1},{3,2},{4,3},{5,4},{6,5},{7,6},{8,7},{9,8},{10,9},{11,1... | collective-permute-start | bytes 25352 | tf_op jit(solution)/shard_map/ppermute | solution.py:24
  639.5 13.9 %collective-permute-start.2 = (f32[12,4,53]{1,2,0:T(8,128)S(1)}, f32[12,4,53]{1,2,0:T(8,128)S(1)}, u32[]{:S(2)}, u32[]{:S(2)}) collective-permute-start(f32[12,4,53]{1,2,0:T(8,128)S(1)} %get-tuple-element.24), channel_id=1, source_target_pairs={{0,32},{32,64},{64,96},{96,128},{128,160},{160,192},{192,224},{224... | collective-permute-start | bytes 30536 | tf_op jit(solution)/shard_map/ppermute | solution.py:23
  644.4 8.9 %collective-permute-start.3 = (f32[12,4,53]{1,2,0:T(8,128)S(1)}, f32[12,4,53]{1,2,0:T(8,128)S(1)}, u32[]{:S(2)}, u32[]{:S(2)}) collective-permute-start(f32[12,4,53]{1,2,0:T(8,128)S(1)} %get-tuple-element.25), channel_id=1, source_target_pairs={{32,0},{64,32},{96,64},{128,96},{160,128},{192,160},{224,192},{256... | collective-permute-start | bytes 30536 | tf_op jit(solution)/shard_map/ppermute | solution.py:24
Sparse Core Ops, SparseCore 0:
  382.4 233.9 all-reduce.1
